TPU v7x, 32 devices: a whole 2x2x4 slice. The times are simulated.
32 devices in a mesh: dp: 8 (over z, y), expert: 4 (over x, core).
Axes of the slice: x: 2, y: 2, z: 4, core: 2. Of those that a mesh axis runs over, the one named last changes fastest.
Arguments:
- tokens: bfloat16 [4096, 1024], P(('dp', 'expert')), may hold values from -6 to 6
- cotangent: bfloat16 [4096, 1024], P(('dp', 'expert')), may hold values from -6 to 6
- expert_ids: int32 [4096, 2], P(('dp', 'expert')), may hold values from 0 to 3, all different within a row; in each aligned block of 128 rows (0 to 127, 128 to 255, ...) at most 128 rows name the same one
- gate_weights: float32 [4096, 2], P(('dp', 'expert')), may hold values from 0.05 to 1
- w_gate: bfloat16 [4, 384, 1024], P('expert'), may hold values from -0.1875 to 0.1875
- w_up: bfloat16 [4, 384, 1024], P('expert'), may hold values from -0.1875 to 0.1875
- w_down: bfloat16 [4, 384, 1024], P('expert'), may hold values from -0.3125 to 0.3125
Outputs:
- layer_out: bfloat16 [4096, 1024], P(('dp', 'expert'))
- grad_tokens: bfloat16 [4096, 1024], P(('dp', 'expert'))
- grad_up: float32 [4, 384, 1024], P('expert', 'dp')
- grad_down: float32 [4, 384, 1024], P('expert', 'dp')
Inputs may be any that keep to these rules, and one draw needn't show every extreme that they name: `expert_ids`: each row names 2 different experts. Among the 128 rows of one device no expert is named more than 128 times, and in every draw some expert is named exactly 128 times by the rows of some device.
All inputs are finite; a program needn't handle non-finite values.
Results may differ from a plain program's by a relative error of at most 0.0065.
Values may be sent and summed in bfloat16 or wider, within the bound.
A program may use at most 64 MiB of HBM per device.

v0:
```python
import jax
import jax.numpy as jnp
from jax import lax
from jax.sharding import PartitionSpec as P


def batched(left_op, right_op, left_dim, right_dim):
    return lax.dot_general(
        left_op,
        right_op,
        (((left_dim,), (right_dim,)), ((0,), (0,))),
        preferred_element_type=jnp.float32,
    )


def forward(received, w_gate, w_up, w_down):
    gate_pre = batched(received, w_gate, 2, 2)
    up_pre = batched(received, w_up, 2, 2)
    gate_sig = jax.nn.sigmoid(gate_pre)
    hidden = (gate_pre * gate_sig * up_pre).astype(jnp.bfloat16)
    expert_out = batched(hidden, w_down, 2, 1).astype(jnp.bfloat16)
    return ((gate_pre, up_pre, gate_sig, hidden), expert_out)


def backward(received, grad_out, saved_acts, w_gate, w_up, w_down):
    gate_pre, up_pre, gate_sig, hidden = saved_acts
    grad_lower = lax.psum_scatter(
        batched(hidden, grad_out, 1, 1), "dp", scatter_dimension=1, tiled=True
    )
    grad_hidden = batched(grad_out, w_down, 2, 2)
    grad_up_pre = (grad_hidden * gate_pre * gate_sig).astype(jnp.bfloat16)
    grad_gate_pre = (grad_hidden * up_pre * gate_sig * (1.0 + gate_pre * (1.0 - gate_sig))).astype(
        jnp.bfloat16
    )
    grad_input = (batched(grad_gate_pre, w_gate, 2, 1) + batched(grad_up_pre, w_up, 2, 1)).astype(
        jnp.bfloat16
    )
    grad_upper = batched(grad_up_pre, received, 1, 1)
    grad_upper = lax.psum_scatter(grad_upper, "dp", scatter_dimension=1, tiled=True)
    return (grad_input, (grad_upper, grad_lower))


def shards(tokens, cotangent, expert_ids, gate_weights, w_gate, w_up, w_down):
    tok_rows, model_width = tokens.shape
    top_count = expert_ids.shape[1]
    local_experts = w_gate.shape[0]
    groups = lax.axis_size("expert")
    experts = local_experts * groups
    capacity = 2 * tok_rows * top_count // experts
    pair_count = tok_rows * top_count
    slot_count = experts * capacity
    flat_ids = expert_ids.reshape(-1)
    flat_gates = gate_weights.reshape(-1)
    onehot = (flat_ids[:, None] == jnp.arange(experts, dtype=jnp.int32)[None, :]).astype(jnp.int32)
    before = jnp.cumsum(onehot, axis=0) - onehot
    slot_rank = jnp.sum(before * onehot, axis=1)
    position = flat_ids * capacity + slot_rank
    matches = position[None, :] == jnp.arange(slot_count, dtype=jnp.int32)[:, None]
    source = (
        jnp.sum(jnp.where(matches, jnp.arange(pair_count, dtype=jnp.int32)[None, :] + 1, 0), axis=1)
        - 1
    )
    filled = source >= 0
    clipped = jnp.maximum(source, 0)
    token_rows = clipped // top_count
    slot_gates = jnp.where(filled, flat_gates[clipped], 0.0)
    sent_tokens = jnp.where(filled[:, None], tokens[token_rows], jnp.zeros((), jnp.bfloat16))
    sent_tokens = sent_tokens.reshape(experts, capacity, model_width)
    sent_grads = (slot_gates[:, None] * cotangent[token_rows].astype(jnp.float32)).astype(
        jnp.bfloat16
    )
    sent_grads = sent_grads.reshape(experts, capacity, model_width)
    received = lax.all_to_all(sent_tokens, "expert", split_axis=0, concat_axis=1, tiled=True)
    saved_acts, expert_out = forward(received, w_gate, w_up, w_down)
    back_out = lax.all_to_all(expert_out, "expert", split_axis=1, concat_axis=0, tiled=True)
    grad_out = lax.all_to_all(sent_grads, "expert", split_axis=0, concat_axis=1, tiled=True)
    grad_input, grads = backward(received, grad_out, saved_acts, w_gate, w_up, w_down)
    back_grad = lax.all_to_all(grad_input, "expert", split_axis=1, concat_axis=0, tiled=True)
    out_rows = (
        back_out.reshape(slot_count, model_width)[position].astype(jnp.float32)
        * flat_gates[:, None]
    )
    layer_out = jnp.sum(out_rows.reshape(tok_rows, top_count, model_width), axis=1).astype(
        jnp.bfloat16
    )
    grad_rows = back_grad.reshape(slot_count, model_width)[position].astype(jnp.float32)
    grad_tokens = jnp.sum(grad_rows.reshape(tok_rows, top_count, model_width), axis=1).astype(
        jnp.bfloat16
    )
    grad_scale = (tok_rows * lax.axis_size("dp") * groups * top_count / experts) ** (-0.5)
    return (layer_out, grad_tokens, grads[0] * grad_scale, grads[1] * grad_scale)


def solution(mesh):
    in_specs = (
        P(("dp", "expert"), None),
        P(("dp", "expert"), None),
        P(("dp", "expert"), None),
        P(("dp", "expert"), None),
        P("expert", None, None),
        P("expert", None, None),
        P("expert", None, None),
    )
    out_specs = (
        P(("dp", "expert"), None),
        P(("dp", "expert"), None),
        P("expert", "dp", None),
        P("expert", "dp", None),
    )
    return jax.shard_map(shards, mesh=mesh, in_specs=in_specs, out_specs=out_specs, check_vma=False)
```

profile of v0, /device:TPU:0, one launch (start us, length us, event | category | flops | bytes accessed | tf_op | source)
XLA Modules:
  0.0 203.4 jit_solution(15513453985991420824)
XLA Ops:
  7.2 0.9 copy.39
  8.4 1.2 reduce-window.6
  10.0 0.2 select_reduce_fusion
  10.2 0.8 copy.45
  11.1 3.5 %gather_fusion.2 = f32[512]{0:T(512)S(1)} fusion(f32[256]{0:T(256)S(1)} %reshape.257, s32[1024]{0:T(1024)S(1)} %pad_clamp_fusion), kind=kCustom, calls=%fused_computation.2 | custom fusion | bytes 6144 | tf_op jit(solution)/shard_map/gather | solution.py:66
  14.7 2.1 %gather_fusion = bf16[512,1024]{1,0:T(8,128)(2,1)S(1)} fusion(bf16[128,1024]{1,0:T(8,128)(2,1)S(1)} %copy-done.1, s32[1024]{0:T(1024)S(1)} %pad_clamp_fusion.2), kind=kCustom, calls=%fused_computation | custom fusion | bytes 2099200 | tf_op jit(solution)/shard_map/gather | solution.py:67
  16.8 1.2 broadcast_select_fusion
  18.0 4.2 %all-to-all-start = ((bf16[4,128,1024]{2,1,0:T(8,128)(2,1)}), bf16[4,128,1024]{2,1,0:T(8,128)(2,1)S(1)}, u32[]{:S(2)}, u32[]{:S(2)}) async-start(bf16[4,128,1024]{2,1,0:T(8,128)(2,1)} %broadcast_select_fusion), calls=%async_computation | async-start | bytes 2097152 | tf_op jit(solution)/shard_map/all_to_all | solution.py:73
  22.2 2.0 %gather_fusion.3 = bf16[512,1024]{1,0:T(8,128)(2,1)S(1)} fusion(bf16[128,1024]{1,0:T(8,128)(2,1)S(1)} %copy-done.2, s32[1024]{0:T(1024)S(1)} %pad_clamp_fusion.2), kind=kCustom, calls=%fused_computation.3 | custom fusion | bytes 2099200 | tf_op jit(solution)/shard_map/gather | solution.py:69
  24.3 1.2 fusion
  25.5 11.1 %all-to-all-done = bf16[4,128,1024]{2,1,0:T(8,128)(2,1)S(1)} async-done(((bf16[4,128,1024]{2,1,0:T(8,128)(2,1)}), bf16[4,128,1024]{2,1,0:T(8,128)(2,1)S(1)}, u32[]{:S(2)}, u32[]{:S(2)}) %all-to-all-start) | async-done | bytes 1048608 | tf_op jit(solution)/shard_map/all_to_all | solution.py:73
  36.6 3.5 %all-to-all-start.2 = ((bf16[4,128,1024]{2,1,0:T(8,128)(2,1)}), bf16[4,128,1024]{2,1,0:T(8,128)(2,1)S(1)}, u32[]{:S(2)}, u32[]{:S(2)}) async-start(bf16[4,128,1024]{2,1,0:T(8,128)(2,1)} %fusion), calls=%async_computation.2 | async-start | bytes 2097152 | tf_op jit(solution)/shard_map/all_to_all | solution.py:76
  40.2 2.9 %fusion.11 = f32[512,384]{1,0:T(8,128)} fusion(bf16[512,1024]{1,0:T(8,128)(2,1)S(1)} %bitcast.83, bf16[1,384,1024]{2,1,0:T(8,128)(2,1)} %param.11), kind=kOutput, calls=%fused_computation.25 | convolution fusion | flops 402653184 | bytes 2621440 | tf_op jit(solution)/shard_map/dot_general | solution.py:8
  43.1 1.6 fusion.7
  44.7 9.8 %all-to-all-done.2 = bf16[4,128,1024]{2,1,0:T(8,128)(2,1)S(1)} async-done(((bf16[4,128,1024]{2,1,0:T(8,128)(2,1)}), bf16[4,128,1024]{2,1,0:T(8,128)(2,1)S(1)}, u32[]{:S(2)}, u32[]{:S(2)}) %all-to-all-start.2) | async-done | bytes 1048608 | tf_op jit(solution)/shard_map/all_to_all | solution.py:76
  54.5 3.0 %multiply_convert_fusion = (bf16[512,384]{1,0:T(8,128)(2,1)S(1)}, bf16[512,384]{1,0:T(8,128)(2,1)S(1)}, f32[512,384]{1,0:T(8,128)}) fusion(f32[512,384]{1,0:T(8,128)} %fusion.11, f32[512,384]{1,0:T(8,128)} %fusion.7, bf16[512,1024]{1,0:T(8,128)(2,1)S(1)} %bitcast.92, bf16[1,384,1024]{2,1,0:T(8,128)(2,1)S(1)} %copy-done), kind=kOutput, calls=%fused_computation.27 | convolution fusion | flops 404422656 | bytes 4980736 | tf_op jit(solution)/shard_map/dot_general | solution.py:8
  57.5 0.8 copy-done.5
  58.3 1.8 convolution_bitcast_fusion
  60.1 0.2 reduce-scatter.3.cloned.1.call-start
  60.4 1.7 convolution_bitcast_fusion.1
  62.1 2.6 %fusion.9 = f32[512,1024]{1,0:T(8,128)S(1)} fusion(bf16[1,384,1024]{2,1,0:T(8,128)(2,1)S(1)} %copy-done.7, f32[512,384]{1,0:T(8,128)} %fusion.11, f32[512,384]{1,0:T(8,128)} %get-tuple-element.10, f32[512,384]{1,0:T(8,128)} %fusion.7), kind=kOutput, calls=%fused_computation.23 | convolution fusion | flops 404619264 | bytes 5242880 | tf_op jit(solution)/shard_map/dot_general | solution.py:8
  64.7 0.7 fusion.2
  65.4 1.6 copy.58
  67.1 0.5 broadcast.255
  67.6 7.8 %reduce.2 = bf16[512,1024]{1,0:T(8,128)(2,1)} reduce(bf16[512,1,1024]{2,1,0:T(2,128)(2,1)S(1)} %bitcast.88, bf16[]{:T(256)} %broadcast.255), dimensions={1}, to_apply=%bitcast.79.reduce_sub_computation | reduce | bytes 2097154
  75.4 3.8 %reshape.318 = bf16[4,2,65536]{2,1,0:T(2,128)(2,1)} reshape(bf16[512,1024]{1,0:T(8,128)(2,1)} %reduce.2) | data formatting | bytes 2097152
  79.2 4.5 %all-to-all-start.3 = ((bf16[4,2,65536]{2,1,0:T(2,128)(2,1)}), bf16[4,2,65536]{2,1,0:T(2,128)(2,1)}, u32[]{:S(2)}, u32[]{:S(2)}) async-start(bf16[4,2,65536]{2,1,0:T(2,128)(2,1)} %reshape.318), calls=%async_computation.3 | async-start | bytes 2097152 | tf_op jit(solution)/shard_map/all_to_all | solution.py:78
  83.7 0.7 fusion.1
  84.4 1.6 copy.59
  86.0 7.8 %reduce.1 = bf16[512,1024]{1,0:T(8,128)(2,1)} reduce(bf16[512,1,1024]{2,1,0:T(2,128)(2,1)S(1)} %bitcast.89, bf16[]{:T(256)} %broadcast.255), dimensions={1}, to_apply=%bitcast.80.reduce_sub_computation | reduce | bytes 2097154
  93.8 3.7 %reshape.316 = bf16[4,2,65536]{2,1,0:T(2,128)(2,1)} reshape(bf16[512,1024]{1,0:T(8,128)(2,1)} %reduce.1) | data formatting | bytes 2097152
  97.6 0.3 all-to-all-done.3
  97.9 3.8 %all-to-all-start.1 = ((bf16[4,2,65536]{2,1,0:T(2,128)(2,1)}), bf16[4,2,65536]{2,1,0:T(2,128)(2,1)S(1)}, u32[]{:S(2)}, u32[]{:S(2)}) async-start(bf16[4,2,65536]{2,1,0:T(2,128)(2,1)} %reshape.316), calls=%async_computation.1 | async-start | bytes 2097152 | tf_op jit(solution)/shard_map/all_to_all | solution.py:75
  102.0 4.0 %reshape.319 = bf16[512,1,1024]{2,1,0:T(2,128)(2,1)} reshape(bf16[4,2,65536]{2,1,0:T(2,128)(2,1)} %all-to-all-done.3) | data formatting | bytes 2097152
  106.0 2.0 copy.56
  108.0 1.2 gather_fusion.4
  109.1 0.2 gather.28
  109.4 6.5 %all-to-all-done.1 = bf16[4,2,65536]{2,1,0:T(2,128)(2,1)S(1)} async-done(((bf16[4,2,65536]{2,1,0:T(2,128)(2,1)}), bf16[4,2,65536]{2,1,0:T(2,128)(2,1)S(1)}, u32[]{:S(2)}, u32[]{:S(2)}) %all-to-all-start.1) | async-done | bytes 1048608 | tf_op jit(solution)/shard_map/all_to_all | solution.py:75
  115.9 2.3 %reshape.317 = bf16[512,1,1024]{2,1,0:T(2,128)(2,1)} reshape(bf16[4,2,65536]{2,1,0:T(2,128)(2,1)S(1)} %all-to-all-done.1) | data formatting | bytes 2097152
  118.2 2.0 copy.57
  120.2 1.2 gather_fusion.1
  121.3 0.7 reshape.260
  122.0 2.1 %reduce_sum.45 = bf16[128,1024]{1,0:T(8,128)(2,1)} reduce(bf16[128,2,1024]{2,1,0:T(2,128)(2,1)S(1)} %gather.28, bf16[]{:T(256)} %constant.37.clone.1), dimensions={1}, to_apply=%region_5.6 | reduce | flops 131072 | bytes 786434 | tf_op jit(solution)/shard_map/reduce_sum | solution.py:87
  124.1 2.1 %multiply_reduce_fusion = bf16[128,1024]{1,0:T(8,128)(2,1)} fusion(f32[128,2,1024]{2,1,0:T(2,128)S(1)} %reshape.260, f32[128,2]{1,0:T(8,128)S(1)} %copy.45), kind=kLoop, calls=%fused_computation.15 | loop fusion | flops 393216 | bytes 1311744 | tf_op jit(solution)/shard_map/reduce_sum | solution.py:83
  126.2 0.9 reduce-scatter.5.cloned.1.call-done
  127.1 1.6 broadcast_multiply_fusion
  128.7 66.2 %reduce-scatter.3.cloned.1.call-done = f32[1,48,1024]{2,1,0:T(8,128)} async-done(((f32[1,384,1024]{2,1,0:T(8,128)}), f32[1,48,1024]{2,1,0:T(8,128)}) %reduce-scatter.3.cloned.1.call-update) | async-done | bytes 196624 | tf_op jit(solution)/shard_map/reduce_scatter | solution.py:39
  194.9 1.6 broadcast_multiply_fusion.1
  (43 shorter events, 1.3 us)
Async XLA Ops:
  7.2 47.4 %copy-start = (bf16[1,384,1024]{2,1,0:T(8,128)(2,1)S(1)}, bf16[1,384,1024]{2,1,0:T(8,128)(2,1)}, u32[]{:S(2)}) copy-start(bf16[1,384,1024]{2,1,0:T(8,128)(2,1)} %param.13) | copy-start | bytes 2359300
  7.2 7.5 %copy-start.1 = (bf16[128,1024]{1,0:T(8,128)(2,1)S(1)}, bf16[128,1024]{1,0:T(8,128)(2,1)}, u32[]{:S(2)}) copy-start(bf16[128,1024]{1,0:T(8,128)(2,1)} %param.7) | copy-start | bytes 786436
  16.8 5.4 %copy-start.2 = (bf16[128,1024]{1,0:T(8,128)(2,1)S(1)}, bf16[128,1024]{1,0:T(8,128)(2,1)}, u32[]{:S(2)}) copy-start(bf16[128,1024]{1,0:T(8,128)(2,1)} %param.8) | copy-start | bytes 786436
  18.0 18.7 %all-to-all-start = ((bf16[4,128,1024]{2,1,0:T(8,128)(2,1)}), bf16[4,128,1024]{2,1,0:T(8,128)(2,1)S(1)}, u32[]{:S(2)}, u32[]{:S(2)}) async-start(bf16[4,128,1024]{2,1,0:T(8,128)(2,1)} %broadcast_select_fusion), calls=%async_computation | async-start | bytes 2097152 | tf_op jit(solution)/shard_map/all_to_all | solution.py:73
  36.6 17.9 %all-to-all-start.2 = ((bf16[4,128,1024]{2,1,0:T(8,128)(2,1)}), bf16[4,128,1024]{2,1,0:T(8,128)(2,1)S(1)}, u32[]{:S(2)}, u32[]{:S(2)}) async-start(bf16[4,128,1024]{2,1,0:T(8,128)(2,1)} %fusion), calls=%async_computation.2 | async-start | bytes 2097152 | tf_op jit(solution)/shard_map/all_to_all | solution.py:76
  40.1 86.9 %reduce-scatter.5.cloned.1.call-start = ((), (), s32[]{:S(2)}) async-start(), calls=%async_computation.7 | async-start | bytes 1769472 | tf_op jit(solution)/shard_map/reduce_scatter | solution.py:27
  40.2 2.9 %copy-start.3 = (bf16[1,384,1024]{2,1,0:T(8,128)(2,1)S(1)}, bf16[1,384,1024]{2,1,0:T(8,128)(2,1)}, u32[]{:S(2)}) copy-start(bf16[1,384,1024]{2,1,0:T(8,128)(2,1)} %param.12) | copy-start | bytes 2359300
  57.5 0.8 copy-start.5
  60.1 134.8 %reduce-scatter.3.cloned.1.call-start = ((), (), s32[]{:S(2)}) async-start(), calls=%async_computation.6 | async-start | bytes 1769472 | tf_op jit(solution)/shard_map/reduce_scatter | solution.py:39
  60.3 1.8 copy-start.7
  62.1 2.6 %copy-start.4 = (bf16[1,384,1024]{2,1,0:T(8,128)(2,1)S(1)}, bf16[1,384,1024]{2,1,0:T(8,128)(2,1)}, u32[]{:S(2)}) copy-start(bf16[1,384,1024]{2,1,0:T(8,128)(2,1)} %param.12) | copy-start | bytes 2359300
  75.4 8.3 %copy-start.6 = (bf16[512,384]{1,0:T(8,128)(2,1)S(1)}, bf16[512,384]{1,0:T(8,128)(2,1)}, u32[]{:S(2)}) copy-start(bf16[512,384]{1,0:T(8,128)(2,1)} %copy-done.5) | copy-start | bytes 1179652
  79.2 18.8 %all-to-all-start.3 = ((bf16[4,2,65536]{2,1,0:T(2,128)(2,1)}), bf16[4,2,65536]{2,1,0:T(2,128)(2,1)}, u32[]{:S(2)}, u32[]{:S(2)}) async-start(bf16[4,2,65536]{2,1,0:T(2,128)(2,1)} %reshape.318), calls=%async_computation.3 | async-start | bytes 2097152 | tf_op jit(solution)/shard_map/all_to_all | solution.py:78
  93.8 7.9 %copy-start.8 = (s32[128,2]{0,1:T(2,128)S(1)}, s32[128,2]{0,1:T(2,128)}, u32[]{:S(2)}) copy-start(s32[128,2]{0,1:T(2,128)} %param.9) | copy-start | bytes 3076
  97.9 17.9 %all-to-all-start.1 = ((bf16[4,2,65536]{2,1,0:T(2,128)(2,1)}), bf16[4,2,65536]{2,1,0:T(2,128)(2,1)S(1)}, u32[]{:S(2)}, u32[]{:S(2)}) async-start(bf16[4,2,65536]{2,1,0:T(2,128)(2,1)} %reshape.316), calls=%async_computation.1 | async-start | bytes 2097152 | tf_op jit(solution)/shard_map/all_to_all | solution.py:75
Sparse Core Ops, SparseCore 0:
  60.2 66.8 reduce-scatter.4
  130.5 64.3 reduce-scatter.2
where the time goes:
time: 204 us; the launch traced here: 203 us
  waiting for transfers between devices  95 us (47%)
  local copies, waits for them, and re-layouts  35.7 us (18%)
  other arithmetic  27 us (13%)
  starting transfers between devices  16.3 us (8%)
  matrix products  15 us (7%)
  between operations  14.3 us (7%)
    reduce_scatter x1, waiting for transfers between devices, backward(): lax.psum_scatter(grad_upper, 'dp', scatter_dimension=1, tiled=True)  66.2 us
    unnamed x27, local copies, waits for them, and re-layouts  20.8 us
    unnamed x3, other arithmetic  15.7 us
    dot_general x8, matrix products, batched(): lax.dot_general(left_op, right_op, (((left_dim,), (right_dim,)), ((0,), (...  15 us
    all_to_all x1, waiting for transfers between devices, shards(): lax.all_to_all(sent_tokens, 'expert', split_axis=0, concat_axis=1, tiled=...  11.1 us
    all_to_all x1, waiting for transfers between devices, shards(): lax.all_to_all(sent_grads, 'expert', split_axis=0, concat_axis=1, tiled=T...  9.83 us
    all_to_all x1, waiting for transfers between devices, shards(): lax.all_to_all(expert_out, 'expert', split_axis=1, concat_axis=0, tiled=T...  6.51 us
    all_to_all x1, starting transfers between devices, shards(): lax.all_to_all(grad_input, 'expert', split_axis=1, concat_axis=0, tiled=T...  4.48 us
  transfers between devices with their start and end apart: 6, of which 6 were waited for; matrix products, arithmetic and copies ran while one was open for 29% of the time, Pallas kernels for 0%

commit v1 on v0

--- a/solution.py
+++ b/solution.py
@@ -70,7 +70,20 @@
         jnp.bfloat16
     )
     sent_grads = sent_grads.reshape(experts, capacity, model_width)
-    received = lax.all_to_all(sent_tokens, "expert", split_axis=0, concat_axis=1, tiled=True)
+    response, fresh = (jax.lax.axis_size("expert"), jax.lax.axis_index("expert"))
+    far_arr = sent_tokens.shape[0] // response
+    e_next = jnp.roll(sent_tokens, shift=-fresh * far_arr, axis=0)
+    nodes = [lax.slice_in_dim(e_next, 0, far_arr, axis=0)]
+    for ix in range(1, response):
+        a_now = lax.slice_in_dim(e_next, ix * far_arr, (ix + 1) * far_arr, axis=0)
+        nodes.append(
+            jax.lax.ppermute(
+                a_now, "expert", [(nth, (nth + ix) % response) for nth in range(response)]
+            )
+        )
+    received = jnp.roll(
+        jnp.concatenate(nodes[::-1], axis=1), (fresh + 1) * nodes[0].shape[1], axis=1
+    )
     saved_acts, expert_out = forward(received, w_gate, w_up, w_down)
     back_out = lax.all_to_all(expert_out, "expert", split_axis=1, concat_axis=0, tiled=True)
     grad_out = lax.all_to_all(sent_grads, "expert", split_axis=0, concat_axis=1, tiled=True)

time: 204 us -> 196 us (0.961)
  waiting for transfers between devices: 95 us -> 81.7 us
  local copies, waits for them, and re-layouts: 35.7 us -> 40.8 us
    reduce_scatter x1, waiting for transfers between devices: 66.2 us -> 0.01 us  [backward(): lax.psum_scatter(grad_upper, 'dp', scatter_dimension=1, tiled=True)]
    reduce_scatter x1, waiting for transfers between devices: 0.94 us -> 66 us  [backward(): lax.psum_scatter(batched(hidden, grad_out, 1, 1), 'dp', scatter_dimension...]
    all_to_all x1 -> x0, waiting for transfers between devices: 11.1 us -> none  [shards(): lax.all_to_all(sent_tokens, 'expert', split_axis=0, concat_axis=1, tiled=...]
    all_to_all x1, waiting for transfers between devices: 9.83 us -> 3.84 us  [shards(): lax.all_to_all(sent_grads, 'expert', split_axis=0, concat_axis=1, tiled=T...]
    ppermute x0 -> x3, waiting for transfers between devices: none -> 4.98 us  [shards(): jax.lax.ppermute(a_now, 'expert', [(nth, (nth + ix) % response) for nth i...]
    all_to_all x1 -> x0, starting transfers between devices: 4.24 us -> none  [shards(): lax.all_to_all(sent_tokens, 'expert', split_axis=0, concat_axis=1, tiled=...]
    unnamed x27 -> x38, local copies, waits for them, and re-layouts: 20.8 us -> 24 us
    ppermute x0 -> x3, starting transfers between devices: none -> 3.2 us  [shards(): jax.lax.ppermute(a_now, 'expert', [(nth, (nth + ix) % response) for nth i...]
  transfers between devices with their start and end apart: 6 -> 8, of which waited for: 6 -> 6; matrix products, arithmetic and copies ran while one was open for 29% -> 33% of each run, Pallas kernels for 0% -> 0%
where the time goes in v1:
time: 196 us; the launch traced here: 195 us
  waiting for transfers between devices  81.7 us (42%)
  local copies, waits for them, and re-layouts  40.8 us (21%)
  other arithmetic  26.4 us (13%)
  starting transfers between devices  15.9 us (8%)
  matrix products  15.5 us (8%)
  between operations  14.5 us (7%)
    reduce_scatter x1, waiting for transfers between devices, backward(): lax.psum_scatter(batched(hidden, grad_out, 1, 1), 'dp', scatter_dimension...  66 us
    unnamed x38, local copies, waits for them, and re-layouts  24 us
    unnamed x3, other arithmetic  15.7 us
    dot_general x8, matrix products, batched(): lax.dot_general(left_op, right_op, (((left_dim,), (right_dim,)), ((0,), (...  15.5 us
    all_to_all x1, waiting for transfers between devices, shards(): lax.all_to_all(expert_out, 'expert', split_axis=1, concat_axis=0, tiled=T...  6.53 us
    ppermute x3, waiting for transfers between devices, shards(): jax.lax.ppermute(a_now, 'expert', [(nth, (nth + ix) % response) for nth i...  4.98 us
    all_to_all x1, starting transfers between devices, shards(): lax.all_to_all(grad_input, 'expert', split_axis=1, concat_axis=0, tiled=T...  4.47 us
    all_to_all x1, starting transfers between devices, shards(): lax.all_to_all(sent_grads, 'expert', split_axis=0, concat_axis=1, tiled=T...  4.23 us
  transfers between devices with their start and end apart: 8, of which 6 were waited for; matrix products, arithmetic and copies ran while one was open for 33% of the time, Pallas kernels for 0%

profile of v1, /device:TPU:0, one launch (start us, length us, event | category | flops | bytes accessed | tf_op | source)
XLA Modules:
  0.0 194.8 jit_solution(16646785315246334690)
XLA Ops:
  7.2 0.9 copy.39
  8.4 1.2 reduce-window.6
  10.2 0.8 copy.45
  11.2 3.5 %gather_fusion.2 = f32[512]{0:T(512)S(1)} fusion(f32[256]{0:T(256)S(1)} %reshape.251, s32[1024]{0:T(1024)S(1)} %pad_clamp_fusion), kind=kCustom, calls=%fused_computation.2 | custom fusion | bytes 6144 | tf_op jit(solution)/shard_map/gather | solution.py:66
  14.7 2.1 %gather_fusion = bf16[512,1024]{1,0:T(8,128)(2,1)S(1)} fusion(bf16[128,1024]{1,0:T(8,128)(2,1)S(1)} %copy-done.1, s32[1024]{0:T(1024)S(1)} %pad_clamp_fusion.2), kind=kCustom, calls=%fused_computation | custom fusion | bytes 2099200 | tf_op jit(solution)/shard_map/gather | solution.py:67
  17.4 1.0 copy-done.3
  18.4 0.9 fusion.29
  19.2 2.4 %collective-permute-start = (bf16[1,128,1024]{2,1,0:T(8,128)(2,1)S(1)}, bf16[1,128,1024]{2,1,0:T(8,128)(2,1)S(1)}, u32[]{:S(2)}, u32[]{:S(2)}) collective-permute-start(bf16[1,128,1024]{2,1,0:T(8,128)(2,1)S(1)} %get-tuple-element.8), channel_id=1, source_target_pairs={{0,3},{1,0},{2,1},{3,2},{4,7},{5,4},{6,5},{7,6},{8,11},{9,8},{10,9... | collective-permute-start | bytes 786440 | tf_op jit(solution)/shard_map/ppermute | solution.py:80
  21.6 0.6 collective-permute-start.1
  22.4 2.0 %gather_fusion.3 = bf16[512,1024]{1,0:T(8,128)(2,1)S(1)} fusion(bf16[128,1024]{1,0:T(8,128)(2,1)S(1)} %copy-done.2, s32[1024]{0:T(1024)S(1)} %pad_clamp_fusion.2), kind=kCustom, calls=%fused_computation.3 | custom fusion | bytes 2099200 | tf_op jit(solution)/shard_map/gather | solution.py:69
  24.5 1.3 fusion
  25.7 4.2 %all-to-all-start.1 = ((bf16[4,128,1024]{2,1,0:T(8,128)(2,1)}), bf16[4,128,1024]{2,1,0:T(8,128)(2,1)}, u32[]{:S(2)}, u32[]{:S(2)}) async-start(bf16[4,128,1024]{2,1,0:T(8,128)(2,1)} %fusion), calls=%async_computation.1 | async-start | bytes 2097152 | tf_op jit(solution)/shard_map/all_to_all | solution.py:89
  30.1 4.8 %collective-permute-done.1 = bf16[1,128,1024]{2,1,0:T(8,128)(2,1)S(1)} collective-permute-done((bf16[1,128,1024]{2,1,0:T(8,128)(2,1)}, bf16[1,128,1024]{2,1,0:T(8,128)(2,1)S(1)}, u32[]{:S(2)}, u32[]{:S(2)}) %collective-permute-start.1) | collective-permute-done | bytes 262176 | tf_op jit(solution)/shard_map/ppermute | solution.py:80
  35.1 1.0 constant_dynamic-update-slice_fusion.3
  36.1 1.0 slice_dynamic-update-slice_fusion
  37.1 1.0 constant_dynamic-update-slice_fusion
  38.1 1.0 slice_dynamic-update-slice_fusion.1
  39.1 1.6 fusion.5
  40.8 1.7 fusion.7
  42.4 3.8 %all-to-all-done.1 = bf16[4,128,1024]{2,1,0:T(8,128)(2,1)} async-done(((bf16[4,128,1024]{2,1,0:T(8,128)(2,1)}), bf16[4,128,1024]{2,1,0:T(8,128)(2,1)}, u32[]{:S(2)}, u32[]{:S(2)}) %all-to-all-start.1) | async-done | bytes 1048608 | tf_op jit(solution)/shard_map/all_to_all | solution.py:89
  46.3 3.5 %multiply_convert_fusion = (bf16[512,384]{1,0:T(8,128)(2,1)S(1)}, bf16[512,384]{1,0:T(8,128)(2,1)}, f32[512,384]{1,0:T(8,128)}) fusion(f32[512,384]{1,0:T(8,128)} %fusion.7, f32[512,384]{1,0:T(8,128)} %fusion.5, bf16[512,1024]{1,0:T(8,128)(2,1)} %bitcast.15, bf16[1,384,1024]{2,1,0:T(8,128)(2,1)S(1)} %copy-done), kind=kOutput, calls=%fused_computation.36 | convolution fusion | flops 404422656 | bytes 4980736 | tf_op jit(solution)/shard_map/dot_general | solution.py:8
  49.7 1.7 convolution_bitcast_fusion.1
  51.8 3.2 %convolution_bitcast_fusion = f32[1,384,1024]{2,1,0:T(8,128)} fusion(bf16[512,384]{1,0:T(8,128)(2,1)} %get-tuple-element.10, bf16[512,1024]{1,0:T(8,128)(2,1)} %bitcast.15), kind=kOutput, calls=%fused_computation.10 | convolution fusion | flops 402653184 | bytes 3014656 | tf_op jit(solution)/shard_map/dot_general | solution.py:8
  55.0 2.3 %fusion.17 = f32[512,1024]{1,0:T(8,128)S(1)} fusion(bf16[1,384,1024]{2,1,0:T(8,128)(2,1)S(1)} %copy-done.8, f32[512,384]{1,0:T(8,128)} %fusion.7, f32[512,384]{1,0:T(8,128)} %get-tuple-element.13, f32[512,384]{1,0:T(8,128)S(1)} %copy-done.9), kind=kOutput, calls=%fused_computation.33 | convolution fusion | flops 404619264 | bytes 5242880 | tf_op jit(solution)/shard_map/dot_general | solution.py:8
  57.4 0.7 fusion.2
  58.1 1.6 copy.58
  59.7 0.5 broadcast.257
  60.2 7.8 %reduce.2 = bf16[512,1024]{1,0:T(8,128)(2,1)} reduce(bf16[512,1,1024]{2,1,0:T(2,128)(2,1)S(1)} %bitcast.88, bf16[]{:T(256)} %broadcast.257), dimensions={1}, to_apply=%bitcast.82.reduce_sub_computation | reduce | bytes 2097154
  68.0 3.8 %reshape.312 = bf16[4,2,65536]{2,1,0:T(2,128)(2,1)} reshape(bf16[512,1024]{1,0:T(8,128)(2,1)} %reduce.2) | data formatting | bytes 2097152
  71.8 4.5 %all-to-all-start.2 = ((bf16[4,2,65536]{2,1,0:T(2,128)(2,1)}), bf16[4,2,65536]{2,1,0:T(2,128)(2,1)}, u32[]{:S(2)}, u32[]{:S(2)}) async-start(bf16[4,2,65536]{2,1,0:T(2,128)(2,1)} %reshape.312), calls=%async_computation.2 | async-start | bytes 2097152 | tf_op jit(solution)/shard_map/all_to_all | solution.py:91
  76.3 0.7 fusion.1
  77.0 1.6 copy.59
  78.6 7.8 %reduce.1 = bf16[512,1024]{1,0:T(8,128)(2,1)} reduce(bf16[512,1,1024]{2,1,0:T(2,128)(2,1)S(1)} %bitcast.89, bf16[]{:T(256)} %broadcast.257), dimensions={1}, to_apply=%bitcast.83.reduce_sub_computation | reduce | bytes 2097154
  86.4 3.8 %reshape.310 = bf16[4,2,65536]{2,1,0:T(2,128)(2,1)} reshape(bf16[512,1024]{1,0:T(8,128)(2,1)} %reduce.1) | data formatting | bytes 2097152
  90.6 3.8 %all-to-all-start = ((bf16[4,2,65536]{2,1,0:T(2,128)(2,1)}), bf16[4,2,65536]{2,1,0:T(2,128)(2,1)S(1)}, u32[]{:S(2)}, u32[]{:S(2)}) async-start(bf16[4,2,65536]{2,1,0:T(2,128)(2,1)} %reshape.310), calls=%async_computation | async-start | bytes 2097152 | tf_op jit(solution)/shard_map/all_to_all | solution.py:88
  94.6 4.0 %reshape.313 = bf16[512,1,1024]{2,1,0:T(2,128)(2,1)} reshape(bf16[4,2,65536]{2,1,0:T(2,128)(2,1)} %all-to-all-done.2) | data formatting | bytes 2097152
  98.6 2.0 %copy.56 = bf16[1,512,1024]{2,1,0:T(8,128)(2,1)S(1)} copy(bf16[1,512,1024]{2,0,1:T(2,128)(2,1)} %bitcast.86) | data formatting | bytes 2097152
  100.6 1.2 gather_fusion.4
  101.9 6.5 %all-to-all-done = bf16[4,2,65536]{2,1,0:T(2,128)(2,1)S(1)} async-done(((bf16[4,2,65536]{2,1,0:T(2,128)(2,1)}), bf16[4,2,65536]{2,1,0:T(2,128)(2,1)S(1)}, u32[]{:S(2)}, u32[]{:S(2)}) %all-to-all-start) | async-done | bytes 1048608 | tf_op jit(solution)/shard_map/all_to_all | solution.py:88
  108.5 2.3 %reshape.311 = bf16[512,1,1024]{2,1,0:T(2,128)(2,1)} reshape(bf16[4,2,65536]{2,1,0:T(2,128)(2,1)S(1)} %all-to-all-done) | data formatting | bytes 2097152
  110.8 2.0 %copy.57 = bf16[1,512,1024]{2,1,0:T(8,128)(2,1)S(1)} copy(bf16[1,512,1024]{2,0,1:T(2,128)(2,1)} %bitcast.87) | data formatting | bytes 2097152
  112.7 1.2 gather_fusion.1
  113.9 0.7 reshape.254
  114.6 2.1 %reduce_sum.45 = bf16[128,1024]{1,0:T(8,128)(2,1)} reduce(bf16[128,2,1024]{2,1,0:T(2,128)(2,1)S(1)} %gather.28, bf16[]{:T(256)} %constant.76.clone.1), dimensions={1}, to_apply=%region_5.6 | reduce | flops 131072 | bytes 786434 | tf_op jit(solution)/shard_map/reduce_sum | solution.py:100
  116.7 2.1 %multiply_reduce_fusion = bf16[128,1024]{1,0:T(8,128)(2,1)} fusion(f32[128,2,1024]{2,1,0:T(2,128)S(1)} %reshape.254, f32[128,2]{1,0:T(8,128)S(1)} %copy.45), kind=kLoop, calls=%fused_computation.23 | loop fusion | flops 393216 | bytes 1311744 | tf_op jit(solution)/shard_map/reduce_sum | solution.py:96
  118.7 1.6 broadcast_multiply_fusion.1
  120.3 66.0 %reduce-scatter.5.cloned.1.call-done = f32[1,48,1024]{2,1,0:T(8,128)} async-done(((f32[1,384,1024]{2,1,0:T(8,128)}), f32[1,48,1024]{2,1,0:T(8,128)}) %reduce-scatter.5.cloned.1.call-update) | async-done | bytes 196624 | tf_op jit(solution)/shard_map/reduce_scatter | solution.py:27
  186.4 1.6 broadcast_multiply_fusion
  (61 shorter events, 3.2 us)
Async XLA Ops:
  7.2 39.1 %copy-start = (bf16[1,384,1024]{2,1,0:T(8,128)(2,1)S(1)}, bf16[1,384,1024]{2,1,0:T(8,128)(2,1)}, u32[]{:S(2)}) copy-start(bf16[1,384,1024]{2,1,0:T(8,128)(2,1)} %param.13) | copy-start | bytes 2359300
  7.2 7.6 %copy-start.1 = (bf16[128,1024]{1,0:T(8,128)(2,1)S(1)}, bf16[128,1024]{1,0:T(8,128)(2,1)}, u32[]{:S(2)}) copy-start(bf16[128,1024]{1,0:T(8,128)(2,1)} %param.7) | copy-start | bytes 786436
  17.0 5.5 %copy-start.2 = (bf16[128,1024]{1,0:T(8,128)(2,1)S(1)}, bf16[128,1024]{1,0:T(8,128)(2,1)}, u32[]{:S(2)}) copy-start(bf16[128,1024]{1,0:T(8,128)(2,1)} %param.8) | copy-start | bytes 786436
  17.4 1.0 copy-start.3
  19.2 10.8 %collective-permute-start = (bf16[1,128,1024]{2,1,0:T(8,128)(2,1)S(1)}, bf16[1,128,1024]{2,1,0:T(8,128)(2,1)S(1)}, u32[]{:S(2)}, u32[]{:S(2)}) collective-permute-start(bf16[1,128,1024]{2,1,0:T(8,128)(2,1)S(1)} %get-tuple-element.8), channel_id=1, source_target_pairs={{0,3},{1,0},{2,1},{3,2},{4,7},{5,4},{6,5},{7,6},{8,11},{9,8},{10,9... | collective-permute-start | bytes 786440 | tf_op jit(solution)/shard_map/ppermute | solution.py:80
  21.6 13.3 %collective-permute-start.1 = (bf16[1,128,1024]{2,1,0:T(8,128)(2,1)}, bf16[1,128,1024]{2,1,0:T(8,128)(2,1)S(1)}, u32[]{:S(2)}, u32[]{:S(2)}) collective-permute-start(bf16[1,128,1024]{2,1,0:T(8,128)(2,1)} %get-tuple-element.7), channel_id=1, source_target_pairs={{0,2},{1,3},{2,0},{3,1},{4,6},{5,7},{6,4},{7,5},{8,10},{9,11},{10,... | collective-permute-start | bytes 786440 | tf_op jit(solution)/shard_map/ppermute | solution.py:80
  22.2 12.9 %collective-permute-start.2 = (bf16[1,128,1024]{2,1,0:T(8,128)(2,1)}, bf16[1,128,1024]{2,1,0:T(8,128)(2,1)}, u32[]{:S(2)}, u32[]{:S(2)}) collective-permute-start(bf16[1,128,1024]{2,1,0:T(8,128)(2,1)} %get-tuple-element.6), channel_id=1, source_target_pairs={{0,1},{1,2},{2,3},{3,0},{4,5},{5,6},{6,7},{7,4},{8,9},{9,10},{10,1... | collective-permute-start | bytes 786440 | tf_op jit(solution)/shard_map/ppermute | solution.py:80
  25.7 20.5 %all-to-all-start.1 = ((bf16[4,128,1024]{2,1,0:T(8,128)(2,1)}), bf16[4,128,1024]{2,1,0:T(8,128)(2,1)}, u32[]{:S(2)}, u32[]{:S(2)}) async-start(bf16[4,128,1024]{2,1,0:T(8,128)(2,1)} %fusion), calls=%async_computation.1 | async-start | bytes 2097152 | tf_op jit(solution)/shard_map/all_to_all | solution.py:89
  30.0 88.8 %reduce-scatter.3.cloned.1.call-start = ((), (), s32[]{:S(2)}) async-start(), calls=%async_computation.5 | async-start | bytes 1769472 | tf_op jit(solution)/shard_map/reduce_scatter | solution.py:39
  30.0 9.1 %copy-start.4 = (bf16[1,384,1024]{2,1,0:T(8,128)(2,1)S(1)}, bf16[1,384,1024]{2,1,0:T(8,128)(2,1)}, u32[]{:S(2)}) copy-start(bf16[1,384,1024]{2,1,0:T(8,128)(2,1)} %param.12) | copy-start | bytes 2359300
  37.1 3.7 %copy-start.7 = (bf16[1,384,1024]{2,1,0:T(8,128)(2,1)S(1)}, bf16[1,384,1024]{2,1,0:T(8,128)(2,1)}, u32[]{:S(2)}) copy-start(bf16[1,384,1024]{2,1,0:T(8,128)(2,1)} %param.11) | copy-start | bytes 2359300
  51.5 134.9 %reduce-scatter.5.cloned.1.call-start = ((), (), s32[]{:S(2)}) async-start(), calls=%async_computation.6 | async-start | bytes 1769472 | tf_op jit(solution)/shard_map/reduce_scatter | solution.py:27
  51.7 3.3 %copy-start.8 = (bf16[1,384,1024]{2,1,0:T(8,128)(2,1)S(1)}, bf16[1,384,1024]{2,1,0:T(8,128)(2,1)}, u32[]{:S(2)}) copy-start(bf16[1,384,1024]{2,1,0:T(8,128)(2,1)} %param.11) | copy-start | bytes 2359300
  51.7 3.3 %copy-start.9 = (f32[512,384]{1,0:T(8,128)S(1)}, f32[512,384]{1,0:T(8,128)}, u32[]{:S(2)}) copy-start(f32[512,384]{1,0:T(8,128)} %fusion.5) | copy-start | bytes 2359300
  55.0 2.3 %copy-start.5 = (bf16[1,384,1024]{2,1,0:T(8,128)(2,1)S(1)}, bf16[1,384,1024]{2,1,0:T(8,128)(2,1)}, u32[]{:S(2)}) copy-start(bf16[1,384,1024]{2,1,0:T(8,128)(2,1)} %param.12) | copy-start | bytes 2359300
  68.0 8.2 %copy-start.6 = (bf16[512,384]{1,0:T(8,128)(2,1)S(1)}, bf16[512,384]{1,0:T(8,128)(2,1)}, u32[]{:S(2)}) copy-start(bf16[512,384]{1,0:T(8,128)(2,1)} %get-tuple-element.10) | copy-start | bytes 1179652
  71.8 18.8 %all-to-all-start.2 = ((bf16[4,2,65536]{2,1,0:T(2,128)(2,1)}), bf16[4,2,65536]{2,1,0:T(2,128)(2,1)}, u32[]{:S(2)}, u32[]{:S(2)}) async-start(bf16[4,2,65536]{2,1,0:T(2,128)(2,1)} %reshape.312), calls=%async_computation.2 | async-start | bytes 2097152 | tf_op jit(solution)/shard_map/all_to_all | solution.py:91
  86.4 7.9 %copy-start.10 = (s32[128,2]{0,1:T(2,128)S(1)}, s32[128,2]{0,1:T(2,128)}, u32[]{:S(2)}) copy-start(s32[128,2]{0,1:T(2,128)} %param.9) | copy-start | bytes 3076
  90.6 17.9 %all-to-all-start = ((bf16[4,2,65536]{2,1,0:T(2,128)(2,1)}), bf16[4,2,65536]{2,1,0:T(2,128)(2,1)S(1)}, u32[]{:S(2)}, u32[]{:S(2)}) async-start(bf16[4,2,65536]{2,1,0:T(2,128)(2,1)} %reshape.310), calls=%async_computation | async-start | bytes 2097152 | tf_op jit(solution)/shard_map/all_to_all | solution.py:88
Sparse Core Ops, SparseCore 0:
  51.6 66.6 reduce-scatter.2
  121.8 64.5 reduce-scatter.4
